TPU v7x, 32 devices: a whole 2x2x4 slice. The times are simulated.
32 devices in a mesh: space: 8 (over y, x, core), mp: 4 (over z).
Axes of the slice: x: 2, y: 2, z: 4, core: 2. Of those that a mesh axis runs over, the one named last changes fastest.
Arguments:
- tokens: bfloat16 [12288, 1024], P('space')
- norm_gain: float32 [1024], replicated, may hold values from 0.5 to 1.5
- w_qkv: bfloat16 [1024, 4, 192], P(None, 'mp')
- w_out: bfloat16 [256, 1024], replicated, may hold values from -0.75 to 0.75
- head_scale: float32 [4], P('mp'), may hold values from 8 to 400
- cycle_to_nested: int32 [12288], P('space'), may hold values from 0 to 12287, as said below
- neighbours: int32 [96, 9], P('space'), may hold values from -1 to 95, as said below
Outputs:
- mixed: bfloat16 [12288, 1024], P(('space', 'mp'))
Inputs may be any that keep to these rules, and one draw needn't show every extreme that they name: `cycle_to_nested`: A permutation of the tokens; the cycle rows of each index of space hold exactly 192 of the nested places of each index of space, the block of 1536 places of that index. `neighbours`: slot 0 names the block itself; the other slots name distinct other blocks at most 6 places away in block order, counted around the end of the order; only slots 7 and 8 may be -1.
All inputs are finite; a program needn't handle non-finite values.
Results may differ from a plain program's by a relative error of at most 0.012.
The roundings to bfloat16 on the way count: a program that leaves them out, or rounds other values in their place, can miss the bound.
Values may be sent and summed in bfloat16 or wider, within the bound.
No kernel may reach another device: no remote copies, remote signals or barrier semaphores. Data moves between devices by JAX's collectives and lax.ppermute only.
A program may use at most 64 MiB of HBM per device.

v0:
```python
import jax
import jax.numpy as jnp
from jax import lax
from jax.sharding import PartitionSpec as P

BLOCK = 128
REACH = 6


def extended_2(shard, sides, width):
    for axis, dim in sides:
        size, length = (lax.axis_size(axis), shard.shape[dim])
        up = [(i, (i + 1) % size) for i in range(size)]
        down = [(j, i) for i, j in up]
        last = lax.slice_in_dim(shard, length - width, length, axis=dim)
        leading = lax.slice_in_dim(shard, 0, width, axis=dim)
        before = lax.ppermute(last, axis, up)
        after = lax.ppermute(leading, axis, down)
        shard = jnp.concatenate([before, shard, after], axis=dim)
    return shard


def norm_rows(tokens, norm_gain):
    values = tokens.astype(jnp.float32)
    mean_square = jnp.mean(values * values, axis=1, keepdims=True)
    return (values * lax.rsqrt(mean_square + 1e-05) * norm_gain).astype(jnp.bfloat16)


def project_head(normed, weight_head, scale_value, head_dim):
    projected = jnp.dot(normed, weight_head, preferred_element_type=jnp.float32)
    query_rows = projected[:, :head_dim]
    key_raw = projected[:, head_dim : 2 * head_dim]
    values = projected[:, 2 * head_dim :]
    query_rows = query_rows * (
        scale_value * lax.rsqrt(jnp.sum(query_rows * query_rows, axis=1, keepdims=True) + 1e-06)
    )
    key_raw = key_raw * lax.rsqrt(jnp.sum(key_raw * key_raw, axis=1, keepdims=True) + 1e-06)
    return jnp.concatenate([query_rows, key_raw, values], axis=1).astype(jnp.bfloat16)


def attend_blocks(query_rows, kv_blocks, positions, present, head_dim):
    block_rows = query_rows.shape[1]
    gathered = kv_blocks[positions]
    batch_blocks = gathered.shape[0]
    gathered_key_rows = gathered[..., :head_dim].reshape(batch_blocks, -1, head_dim)
    gathered_value_rows = gathered[..., head_dim:].reshape(batch_blocks, -1, head_dim)
    score_matrix = jnp.einsum(
        "ltv,lpv->ltp", query_rows, gathered_key_rows, preferred_element_type=jnp.float32
    )
    key_mask = jnp.repeat(present, block_rows, axis=1)[:, None, :]
    score_matrix = jnp.where(key_mask, score_matrix, -1e30)
    row_max = jnp.max(score_matrix, axis=2, keepdims=True)
    exponent = jnp.exp(score_matrix - row_max)
    row_total = jnp.sum(exponent, axis=2, keepdims=True)
    attention_weight = exponent.astype(jnp.bfloat16)
    weighted_sum = jnp.einsum(
        "uct,uth->uch", attention_weight, gathered_value_rows, preferred_element_type=jnp.float32
    )
    return (weighted_sum / row_total).astype(jnp.bfloat16)


def per_device(tokens, norm_gain, w_qkv, w_out, head_scale, cycle_to_nested, neighbours):
    tok_dev, model_width = tokens.shape
    space_count = lax.axis_size("space")
    head_dim = w_qkv.shape[2] // 3
    weight_head = w_qkv.reshape(model_width, 3 * head_dim)
    normed = norm_rows(tokens, norm_gain)
    row_order = jnp.argsort(cycle_to_nested)
    group_rows = tok_dev // space_count
    send_slots = cycle_to_nested[row_order].reshape(space_count, group_rows)
    base_slot = lax.axis_index("space") * tok_dev
    packed = project_head(normed, weight_head, head_scale[0], head_dim)
    send_rows = packed[row_order].reshape(space_count, group_rows, 3 * head_dim)
    got_rows, got_slots = (
        lax.all_to_all(send_rows, "space", split_axis=0, concat_axis=0, tiled=True),
        lax.all_to_all(send_slots, "space", split_axis=0, concat_axis=0, tiled=True),
    )
    slot_local = got_slots.reshape(-1) - base_slot
    nested_ordering = (
        jnp.zeros_like(packed).at[slot_local].set(got_rows.reshape(tok_dev, 3 * head_dim))
    )
    query_rows = nested_ordering[:, :head_dim].reshape(-1, BLOCK, head_dim)
    key_vals = nested_ordering[:, head_dim:]
    blk_count = tok_dev // BLOCK
    padding_blocks = REACH
    extended = extended_2(key_vals, (("space", 0),), REACH * BLOCK)
    kv_blocks = extended.reshape(blk_count + 2 * padding_blocks, BLOCK, 2 * head_dim)
    cycle_blocks = blk_count * space_count
    half_cycle = cycle_blocks // 2
    relative = (
        jnp.mod(neighbours - lax.axis_index("space") * blk_count + half_cycle, cycle_blocks)
        - half_cycle
    )
    present = neighbours >= 0
    positions = jnp.where(present, relative + padding_blocks, 0)
    attn = attend_blocks(query_rows, kv_blocks, positions, present, head_dim).reshape(
        tok_dev, head_dim
    )
    head_rows = lax.all_to_all(attn, "mp", split_axis=0, concat_axis=1, tiled=True)
    return jnp.dot(head_rows, w_out, preferred_element_type=jnp.float32).astype(jnp.bfloat16)


def solution(mesh):
    placed = (
        P("space", None),
        P(),
        P(None, "mp", None),
        P(),
        P("mp"),
        P("space"),
        P("space", None),
    )
    return jax.shard_map(
        per_device, mesh=mesh, in_specs=placed, out_specs=P(("space", "mp"), None), check_vma=False
    )
```

profile of v0, /device:TPU:0, one launch (start us, length us, event | category | flops | bytes accessed | tf_op | source)
XLA Modules:
  0.0 90.3 jit_solution(2709928269623220711)
XLA Ops:
  0.0 0.0 copy-start
  0.0 0.0 copy-start.1
  0.0 5.8 %sort.17 = (s32[1536]{0:T(1024)}, s32[1536]{0:T(1024)S(1)}) sort(s32[1536]{0:T(1024)} %param.12, s32[1536]{0:T(1024)S(1)} %iota.4), dimensions={0}, to_apply=%region_0.0 | sort | flops 16896 | bytes 24576 | tf_op jit(solution)/shard_map/jit(argsort)/sort | solution.py:68
  5.8 0.0 copy-done.1
  5.8 0.0 copy-start.4
  5.8 0.0 copy-start.5
  5.9 8.4 %gather_fusion = s32[1536]{0:T(1024)S(1)} fusion(s32[1536]{0:T(1024)S(1)} %copy-done.1, s32[2048]{0:T(1024)S(1)} %pad_clamp_fusion), kind=kCustom, calls=%fused_computation | custom fusion | bytes 18432 | tf_op jit(solution)/shard_map/gather | solution.py:70
  14.2 0.7 all_to_all.23
  14.9 5.2 %all-to-all-start = ((s32[8,1,192]{2,1,0:T(1,128)}), s32[8,1,192]{2,1,0:T(1,128)S(1)}, u32[]{:S(2)}, u32[]{:S(2)}) async-start(s32[8,1,192]{2,1,0:T(1,128)} %all_to_all.23), calls=%async_computation | async-start | bytes 16384 | tf_op jit(solution)/shard_map/all_to_all | solution.py:76
  20.1 2.6 %fusion = f32[1536]{0:T(1024)S(1)} fusion(bf16[1536,1024]{1,0:T(8,128)(2,1)} %param.7), kind=kLoop, calls=%fused_computation.8 | loop fusion | flops 4717056 | bytes 3151872 | tf_op jit(solution)/shard_map/reduce_sum | solution.py:25
  22.7 0.0 copy-done.4
  22.7 0.0 copy-done.5
  22.7 3.2 %fusion.10 = f32[1536,192]{0,1:T(8,128)S(1)} fusion(bf16[1536,1024]{1,0:T(8,128)(2,1)} %param.7, f32[1024]{0:T(1024)S(1)} %copy-done.5, f32[1536]{0:T(1024)S(1)} %add_rsqrt_fusion.1, bf16[1024,1,192]{0,2,1:T(8,128)(2,1)S(1)} %copy-done.4), kind=kOutput, calls=%fused_computation.17 | convolution fusion | flops 610271232 | bytes 4728832 | tf_op jit(solution)/shard_map/dot_general | solution.py:30
  25.9 0.1 multiply_reduce_fusion.1
  26.7 0.1 multiply_convert_fusion.1
  26.8 0.3 copy.23
  27.1 0.0 copy-start.3
  27.1 5.4 %gather_fusion.1 = bf16[1536,192]{1,0:T(8,128)(2,1)} fusion(bf16[1536,192]{1,0:T(8,128)(2,1)S(1)} %copy.23, s32[2048]{0:T(1024)S(1)} %pad_clamp_fusion), kind=kCustom, calls=%fused_computation.1 | custom fusion | bytes 1185792 | tf_op jit(solution)/shard_map/gather | solution.py:73
  32.4 0.0 all-to-all-done
  32.4 4.2 %all-to-all-start.1 = ((bf16[8,192,192]{2,1,0:T(8,128)(2,1)}), bf16[8,192,192]{2,1,0:T(8,128)(2,1)S(1)}, u32[]{:S(2)}, u32[]{:S(2)}) async-start(bf16[8,192,192]{2,1,0:T(8,128)(2,1)} %bitcast.2), calls=%async_computation.1 | async-start | bytes 1572864 | tf_op jit(solution)/shard_map/all_to_all | solution.py:75
  36.6 0.0 copy-done.3
  36.7 0.1 sub.33
  36.8 12.4 %all-to-all-done.1 = bf16[8,192,192]{2,1,0:T(8,128)(2,1)S(1)} async-done(((bf16[8,192,192]{2,1,0:T(8,128)(2,1)}), bf16[8,192,192]{2,1,0:T(8,128)(2,1)S(1)}, u32[]{:S(2)}, u32[]{:S(2)}) %all-to-all-start.1) | async-done | bytes 589856 | tf_op jit(solution)/shard_map/all_to_all | solution.py:75
  49.2 7.3 %scatter_custom_fusion = bf16[1536,192]{1,0:T(8,128)(2,1)S(1)} fusion(s32[1536]{0:T(1024)S(1)} %fusion.25, bf16[1536,192]{1,0:T(8,128)(2,1)S(1)} %bitcast.31, bf16[]{:T(256)} %constant.17.clone.1), kind=kCustom, calls=%fused_computation.31 | custom fusion | bytes 589826 | tf_op jit(solution)/shard_map/scatter | solution.py:80
  56.5 0.0 copy-start.2
  56.5 0.2 fusion.28
  56.7 0.1 collective-permute-start
  56.8 2.6 %collective-permute-start.1 = (bf16[768,128]{1,0:T(8,128)(2,1)S(1)}, bf16[768,128]{1,0:T(8,128)(2,1)S(1)}, u32[]{:S(2)}, u32[]{:S(2)}) collective-permute-start(bf16[768,128]{1,0:T(8,128)(2,1)S(1)} %get-tuple-element.14), channel_id=1, source_target_pairs={{4,0},{8,4},{12,8},{16,12},{20,16},{24,20},{28,24},{0,28},{5,1},{9... | collective-permute-start | bytes 589832 | tf_op jit(solution)/shard_map/ppermute | solution.py:18
  59.4 0.1 reshape.104
  59.5 0.1 broadcast_in_dim.36
  59.7 0.2 slice.50
  59.8 5.0 %collective-permute-done = bf16[768,128]{1,0:T(8,128)(2,1)S(1)} collective-permute-done((bf16[768,128]{1,0:T(8,128)(2,1)S(1)}, bf16[768,128]{1,0:T(8,128)(2,1)S(1)}, u32[]{:S(2)}, u32[]{:S(2)}) %collective-permute-start) | collective-permute-done | bytes 196640 | tf_op jit(solution)/shard_map/ppermute | solution.py:17
  64.8 0.0 collective-permute-done.1
  64.8 0.1 pad_maximum_fusion
  64.9 2.8 %gather_fusion.2 = bf16[108,128,128]{2,1,0:T(8,128)(2,1)} fusion(bf16[24,128,128]{2,1,0:T(8,128)(2,1)S(1)} %bitcast.27, s32[1024]{0:T(1024)S(1)} %pad_clamp_fusion.1), kind=kCustom, calls=%fused_computation.2 | custom fusion | bytes 7078320 | tf_op jit(solution)/shard_map/gather | solution.py:43
  67.7 0.0 copy-done.2
  67.7 0.0 slice-start
  67.7 4.5 %fusion.27 = (bf16[12,9,128,64]{3,2,1,0:T(8,128)(2,1)S(1)}, bf16[12,9,128,64]{3,2,1,0:T(8,128)(2,1)S(1)}) fusion(bf16[12,9,128,128]{3,2,1,0:T(8,128)(2,1)} %bitcast.26), kind=kLoop, calls=%fused_computation.49 | loop fusion | bytes 7077888 | tf_op jit(solution)/shard_map/slice | solution.py:45
  72.2 0.0 slice-done
  72.2 1.3 %select_reduce_fusion = (f32[12,128]{1,0:T(8,128)S(1)}, f32[12,128,1152]{2,1,0:T(8,128)S(1)}) fusion(pred[12,1152]{1,0:T(8,128)(4,1)S(1)} %bitcast.33, bf16[12,128,64]{2,1,0:T(8,128)(2,1)S(1)} %bitcast.29, bf16[12,1152,64]{2,1,0:T(8,128)(2,1)S(1)} %bitcast.28), kind=kOutput, calls=%fused_computation.7 | convolution fusion | flops 230029824 | bytes 9063936 | tf_op jit(solution)/shard_map/ltv,lpv->ltp/dot_general | solution.py:47
  73.5 1.7 %fusion.3 = f32[12,128]{1,0:T(8,128)S(1)} fusion(f32[12,128,1152]{2,1,0:T(8,128)S(1)} %get-tuple-element.16, f32[12,128]{1,0:T(8,128)S(1)} %get-tuple-element.15, pred[12,1152]{1,0:T(8,128)(4,1)S(1)} %bitcast.34), kind=kLoop, calls=%fused_computation.11 | loop fusion | flops 5306880 | bytes 7104000 | tf_op jit(solution)/shard_map/reduce_sum | solution.py:54
  75.2 2.0 %fusion.17 = bf16[12,128,64]{1,2,0:T(8,128)(2,1)S(1)} fusion(bf16[12,1152,64]{2,1,0:T(8,128)(2,1)S(1)} %bitcast.30, f32[12,128,1152]{2,1,0:T(8,128)S(1)} %get-tuple-element.16, f32[12,128]{1,0:T(8,128)S(1)} %get-tuple-element.15, pred[12,1152]{1,0:T(8,128)(4,1)S(1)} %bitcast.35, f32[12,128]{1,0:T(8,128)S(1)} %fusion.3), kind=kOutput, calls=%fused_computation.22 | convolution fusion | flops 231997440 | bytes 9070080 | tf_op jit(solution)/shard_map/uct,uth->uch/dot_general | solution.py:56
  77.2 0.1 copy.28
  77.3 0.1 all_to_all.26
  77.5 11.6 %all_to_all.33 = bf16[4,384,64]{1,2,0:T(8,128)(2,1)S(1)} all-to-all(bf16[4,384,64]{1,2,0:T(8,128)(2,1)S(1)} %copy.29), channel_id=1, replica_groups=mesh['space'=8,'mp'=4] {'mp'}, dimensions={0} | all-to-all | bytes 393216 | tf_op jit(solution)/shard_map/all_to_all | solution.py:99
  89.1 0.0 copy-done
  89.1 1.3 %convolution_convert_fusion = bf16[384,1024]{1,0:T(8,128)(2,1)} fusion(bf16[384,256]{0,1:T(8,128)(2,1)S(1)} %bitcast.32, bf16[256,1024]{1,0:T(8,128)(2,1)S(1)} %copy-done), kind=kOutput, calls=%fused_computation.20 | convolution fusion | flops 201719808 | bytes 1507328 | tf_op jit(solution)/shard_map/dot_general | solution.py:100
  (15 shorter events, 0.2 us)
Async XLA Ops:
  0.0 89.1 %copy-start = (bf16[256,1024]{1,0:T(8,128)(2,1)S(1)}, bf16[256,1024]{1,0:T(8,128)(2,1)}, u32[]{:S(2)}) copy-start(bf16[256,1024]{1,0:T(8,128)(2,1)} %param.10) | copy-start | bytes 1572868
  0.0 5.8 %copy-start.1 = (s32[1536]{0:T(1024)S(1)}, s32[1536]{0:T(1024)}, u32[]{:S(2)}) copy-start(s32[1536]{0:T(1024)} %param.12) | copy-start | bytes 18436
  5.8 16.9 %copy-start.4 = (bf16[1024,1,192]{0,2,1:T(8,128)(2,1)S(1)}, bf16[1024,1,192]{0,2,1:T(8,128)(2,1)}, u32[]{:S(2)}) copy-start(bf16[1024,1,192]{0,2,1:T(8,128)(2,1)} %param.9) | copy-start | bytes 1179652
  5.8 16.9 %copy-start.5 = (f32[1024]{0:T(1024)S(1)}, f32[1024]{0:T(1024)}, u32[]{:S(2)}) copy-start(f32[1024]{0:T(1024)} %param.8) | copy-start | bytes 12292
  14.9 17.5 %all-to-all-start = ((s32[8,1,192]{2,1,0:T(1,128)}), s32[8,1,192]{2,1,0:T(1,128)S(1)}, u32[]{:S(2)}, u32[]{:S(2)}) async-start(s32[8,1,192]{2,1,0:T(1,128)} %all_to_all.23), calls=%async_computation | async-start | bytes 16384 | tf_op jit(solution)/shard_map/all_to_all | solution.py:76
  27.1 9.6 %copy-start.3 = (s32[12,9]{1,0:T(8,128)S(1)}, s32[12,9]{1,0:T(8,128)}, u32[]{:S(2)}) copy-start(s32[12,9]{1,0:T(8,128)} %param.13) | copy-start | bytes 1300
  32.4 16.8 %all-to-all-start.1 = ((bf16[8,192,192]{2,1,0:T(8,128)(2,1)}), bf16[8,192,192]{2,1,0:T(8,128)(2,1)S(1)}, u32[]{:S(2)}, u32[]{:S(2)}) async-start(bf16[8,192,192]{2,1,0:T(8,128)(2,1)} %bitcast.2), calls=%async_computation.1 | async-start | bytes 1572864 | tf_op jit(solution)/shard_map/all_to_all | solution.py:75
  56.5 11.2 %copy-start.2 = (bf16[1536,192]{1,0:T(8,128)(2,1)}, bf16[1536,192]{1,0:T(8,128)(2,1)S(1)}, u32[]{:S(2)}) copy-start(bf16[1536,192]{1,0:T(8,128)(2,1)S(1)} %scatter_custom_fusion) | copy-start | bytes 1769476
  56.7 8.1 %collective-permute-start = (bf16[768,128]{1,0:T(8,128)(2,1)S(1)}, bf16[768,128]{1,0:T(8,128)(2,1)S(1)}, u32[]{:S(2)}, u32[]{:S(2)}) collective-permute-start(bf16[768,128]{1,0:T(8,128)(2,1)S(1)} %get-tuple-element.13), channel_id=1, source_target_pairs={{0,4},{4,8},{8,12},{12,16},{16,20},{20,24},{24,28},{28,0},{1,5},{5... | collective-permute-start | bytes 589832 | tf_op jit(solution)/shard_map/ppermute | solution.py:17
  56.8 8.1 %collective-permute-start.1 = (bf16[768,128]{1,0:T(8,128)(2,1)S(1)}, bf16[768,128]{1,0:T(8,128)(2,1)S(1)}, u32[]{:S(2)}, u32[]{:S(2)}) collective-permute-start(bf16[768,128]{1,0:T(8,128)(2,1)S(1)} %get-tuple-element.14), channel_id=1, source_target_pairs={{4,0},{8,4},{12,8},{16,12},{20,16},{24,20},{28,24},{0,28},{5,1},{9... | collective-permute-start | bytes 589832 | tf_op jit(solution)/shard_map/ppermute | solution.py:18
  67.7 4.5 %slice-start = ((bf16[1536,192]{1,0:T(8,128)(2,1)}), bf16[1536,64]{1,0:T(8,128)(2,1)S(1)}, s32[]{:S(2)}) async-start(bf16[1536,192]{1,0:T(8,128)(2,1)} %copy-done.2), calls=%async_computation.3 | async-start | bytes 786432 | tf_op jit(solution)/shard_map/slice | solution.py:82
where the time goes:
time: 90.7 us; the launch traced here: 90.3 us
  local copies, waits for them, and re-layouts  30.3 us (33%)
  waiting for transfers between devices  17.4 us (19%)
  starting transfers between devices  12.1 us (13%)
  blocking collectives  11.6 us (13%)
  other arithmetic  10.4 us (11%)
  matrix products  7.71 us (9%)
  between operations  0.91 us (1%)
    all_to_all x1, waiting for transfers between devices, per_device(): lax.all_to_all(send_rows, 'space', split_axis=0, concat_axis=0, tiled=True)  12.4 us
    all_to_all x1, blocking collectives, per_device(): lax.all_to_all(attn, 'mp', split_axis=0, concat_axis=1, tiled=True)  11.6 us
    gather x1, local copies, waits for them, and re-layouts, per_device(): send_slots = cycle_to_nested[row_order].reshape(space_count, group_rows)  8.39 us
    scatter x1, local copies, waits for them, and re-layouts, per_device(): jnp.zeros_like(packed).at[slot_local]  7.32 us
    sort x1, other arithmetic, per_device(): row_order = jnp.argsort(cycle_to_nested)  5.8 us
    gather x1, local copies, waits for them, and re-layouts, per_device(): send_rows = packed[row_order].reshape(space_count, group_rows, 3 * head_dim)  5.36 us
    all_to_all x1, starting transfers between devices, per_device(): lax.all_to_all(send_slots, 'space', split_axis=0, concat_axis=0, tiled=True)  5.2 us
    ppermute x1, waiting for transfers between devices, extended_2(): before = lax.ppermute(last, axis, up)  4.99 us
  transfers between devices with their start and end apart: 4, of which 2 were waited for; matrix products, arithmetic and copies ran while one was open for 13% of the time, Pallas kernels for 0%

commit v1 on v0

--- a/solution.py
+++ b/solution.py
@@ -96,7 +96,9 @@
     attn = attend_blocks(query_rows, kv_blocks, positions, present, head_dim).reshape(
         tok_dev, head_dim
     )
-    head_rows = lax.all_to_all(attn, "mp", split_axis=0, concat_axis=1, tiled=True)
+    head_rows = jnp.concatenate(
+        lax.all_to_all(jnp.stack(jnp.split(attn, lax.axis_size("mp"), axis=0)), "mp", 0, 0), axis=1
+    )
     return jnp.dot(head_rows, w_out, preferred_element_type=jnp.float32).astype(jnp.bfloat16)
 
 

time: 90.7 us -> 90.9 us (level)
  no operation moved by 1% of the time
where the time goes in v1:
time: 90.9 us; the launch traced here: 90.5 us
  local copies, waits for them, and re-layouts  30.4 us (33%)
  waiting for transfers between devices  17.4 us (19%)
  starting transfers between devices  12.1 us (13%)
  blocking collectives  11.6 us (13%)
  other arithmetic  10.4 us (11%)
  matrix products  7.71 us (8%)
  between operations  0.94 us (1%)
    all_to_all x1, waiting for transfers between devices, per_device(): lax.all_to_all(send_rows, 'space', split_axis=0, concat_axis=0, tiled=True)  12.4 us
    all_to_all x1, blocking collectives, per_device(): lax.all_to_all(jnp.stack(jnp.split(attn, lax.axis_size('mp'), axis=0)), '...  11.6 us
    gather x1, local copies, waits for them, and re-layouts, per_device(): send_slots = cycle_to_nested[row_order].reshape(space_count, group_rows)  8.39 us
    scatter x1, local copies, waits for them, and re-layouts, per_device(): jnp.zeros_like(packed).at[slot_local]  7.32 us
    sort x1, other arithmetic, per_device(): row_order = jnp.argsort(cycle_to_nested)  5.8 us
    gather x1, local copies, waits for them, and re-layouts, per_device(): send_rows = packed[row_order].reshape(space_count, group_rows, 3 * head_dim)  5.36 us
    all_to_all x1, starting transfers between devices, per_device(): lax.all_to_all(send_slots, 'space', split_axis=0, concat_axis=0, tiled=True)  5.2 us
    ppermute x1, waiting for transfers between devices, extended_2(): before = lax.ppermute(last, axis, up)  4.99 us
  transfers between devices with their start and end apart: 4, of which 2 were waited for; matrix products, arithmetic and copies ran while one was open for 13% of the time, Pallas kernels for 0%

profile of v1, /device:TPU:0, one launch (start us, length us, event | category | flops | bytes accessed | tf_op | source)
XLA Modules:
  0.0 90.5 jit_solution(6265551992363898701)
XLA Ops:
  0.0 0.0 copy-start
  0.0 0.0 copy-start.1
  0.0 5.8 %sort.17 = (s32[1536]{0:T(1024)}, s32[1536]{0:T(1024)S(1)}) sort(s32[1536]{0:T(1024)} %param.12, s32[1536]{0:T(1024)S(1)} %iota.4), dimensions={0}, to_apply=%region_0.0 | sort | flops 16896 | bytes 24576 | tf_op jit(solution)/shard_map/jit(argsort)/sort | solution.py:68
  5.8 0.0 copy-done.1
  5.8 0.0 copy-start.4
  5.8 0.0 copy-start.5
  5.9 8.4 %gather_fusion = s32[1536]{0:T(1024)S(1)} fusion(s32[1536]{0:T(1024)S(1)} %copy-done.1, s32[2048]{0:T(1024)S(1)} %pad_clamp_fusion), kind=kCustom, calls=%fused_computation | custom fusion | bytes 18432 | tf_op jit(solution)/shard_map/gather | solution.py:70
  14.2 0.7 all_to_all.12
  14.9 5.2 %all-to-all-start = ((s32[8,1,192]{2,1,0:T(1,128)}), s32[8,1,192]{2,1,0:T(1,128)S(1)}, u32[]{:S(2)}, u32[]{:S(2)}) async-start(s32[8,1,192]{2,1,0:T(1,128)} %all_to_all.12), calls=%async_computation | async-start | bytes 16384 | tf_op jit(solution)/shard_map/all_to_all | solution.py:76
  20.1 2.6 %fusion = f32[1536]{0:T(1024)S(1)} fusion(bf16[1536,1024]{1,0:T(8,128)(2,1)} %param.7), kind=kLoop, calls=%fused_computation.8 | loop fusion | flops 4717056 | bytes 3151872 | tf_op jit(solution)/shard_map/reduce_sum | solution.py:25
  22.7 0.0 copy-done.4
  22.7 0.0 copy-done.5
  22.7 3.2 %fusion.10 = f32[1536,192]{0,1:T(8,128)S(1)} fusion(bf16[1536,1024]{1,0:T(8,128)(2,1)} %param.7, f32[1024]{0:T(1024)S(1)} %copy-done.5, f32[1536]{0:T(1024)S(1)} %add_rsqrt_fusion.1, bf16[1024,1,192]{0,2,1:T(8,128)(2,1)S(1)} %copy-done.4), kind=kOutput, calls=%fused_computation.17 | convolution fusion | flops 610271232 | bytes 4728832 | tf_op jit(solution)/shard_map/dot_general | solution.py:30
  25.9 0.1 multiply_reduce_fusion.1
  26.7 0.1 multiply_convert_fusion.1
  26.8 0.3 copy.18
  27.1 0.0 copy-start.3
  27.1 5.4 %gather_fusion.1 = bf16[1536,192]{1,0:T(8,128)(2,1)} fusion(bf16[1536,192]{1,0:T(8,128)(2,1)S(1)} %copy.18, s32[2048]{0:T(1024)S(1)} %pad_clamp_fusion), kind=kCustom, calls=%fused_computation.1 | custom fusion | bytes 1185792 | tf_op jit(solution)/shard_map/gather | solution.py:73
  32.4 0.0 all-to-all-done
  32.4 4.2 %all-to-all-start.1 = ((bf16[8,192,192]{2,1,0:T(8,128)(2,1)}), bf16[8,192,192]{2,1,0:T(8,128)(2,1)S(1)}, u32[]{:S(2)}, u32[]{:S(2)}) async-start(bf16[8,192,192]{2,1,0:T(8,128)(2,1)} %bitcast.2), calls=%async_computation.1 | async-start | bytes 1572864 | tf_op jit(solution)/shard_map/all_to_all | solution.py:75
  36.6 0.0 copy-done.3
  36.7 0.1 sub.33
  36.8 12.4 %all-to-all-done.1 = bf16[8,192,192]{2,1,0:T(8,128)(2,1)S(1)} async-done(((bf16[8,192,192]{2,1,0:T(8,128)(2,1)}), bf16[8,192,192]{2,1,0:T(8,128)(2,1)S(1)}, u32[]{:S(2)}, u32[]{:S(2)}) %all-to-all-start.1) | async-done | bytes 589856 | tf_op jit(solution)/shard_map/all_to_all | solution.py:75
  49.2 7.3 %scatter_custom_fusion = bf16[1536,192]{1,0:T(8,128)(2,1)S(1)} fusion(s32[1536]{0:T(1024)S(1)} %fusion.25, bf16[1536,192]{1,0:T(8,128)(2,1)S(1)} %bitcast.37, bf16[]{:T(256)} %constant.17.clone.1), kind=kCustom, calls=%fused_computation.31 | custom fusion | bytes 589826 | tf_op jit(solution)/shard_map/scatter | solution.py:80
  56.5 0.0 copy-start.2
  56.5 0.2 fusion.28
  56.7 0.1 collective-permute-start
  56.8 2.6 %collective-permute-start.1 = (bf16[768,128]{1,0:T(8,128)(2,1)S(1)}, bf16[768,128]{1,0:T(8,128)(2,1)S(1)}, u32[]{:S(2)}, u32[]{:S(2)}) collective-permute-start(bf16[768,128]{1,0:T(8,128)(2,1)S(1)} %get-tuple-element.14), channel_id=1, source_target_pairs={{4,0},{8,4},{12,8},{16,12},{20,16},{24,20},{28,24},{0,28},{5,1},{9... | collective-permute-start | bytes 589832 | tf_op jit(solution)/shard_map/ppermute | solution.py:18
  59.4 0.1 reshape.116
  59.5 0.1 broadcast_in_dim.36
  59.7 0.2 slice.54
  59.8 5.0 %collective-permute-done = bf16[768,128]{1,0:T(8,128)(2,1)S(1)} collective-permute-done((bf16[768,128]{1,0:T(8,128)(2,1)S(1)}, bf16[768,128]{1,0:T(8,128)(2,1)S(1)}, u32[]{:S(2)}, u32[]{:S(2)}) %collective-permute-start) | collective-permute-done | bytes 196640 | tf_op jit(solution)/shard_map/ppermute | solution.py:17
  64.8 0.0 collective-permute-done.1
  64.8 0.1 pad_maximum_fusion
  64.9 2.8 %gather_fusion.2 = bf16[108,128,128]{2,1,0:T(8,128)(2,1)} fusion(bf16[24,128,128]{2,1,0:T(8,128)(2,1)S(1)} %bitcast.33, s32[1024]{0:T(1024)S(1)} %pad_clamp_fusion.1), kind=kCustom, calls=%fused_computation.2 | custom fusion | bytes 7078320 | tf_op jit(solution)/shard_map/gather | solution.py:43
  67.7 0.0 copy-done.2
  67.7 4.5 %fusion.27 = (bf16[12,9,128,64]{3,2,1,0:T(8,128)(2,1)S(1)}, bf16[12,9,128,64]{3,2,1,0:T(8,128)(2,1)S(1)}) fusion(bf16[12,9,128,128]{3,2,1,0:T(8,128)(2,1)} %bitcast.32), kind=kLoop, calls=%fused_computation.50 | loop fusion | bytes 7077888 | tf_op jit(solution)/shard_map/slice | solution.py:45
  72.2 0.0 slice-done
  72.2 1.3 %select_reduce_fusion = (f32[12,128]{1,0:T(8,128)S(1)}, f32[12,128,1152]{2,1,0:T(8,128)S(1)}) fusion(pred[12,1152]{1,0:T(8,128)(4,1)S(1)} %bitcast.39, bf16[12,128,64]{2,1,0:T(8,128)(2,1)S(1)} %bitcast.35, bf16[12,1152,64]{2,1,0:T(8,128)(2,1)S(1)} %bitcast.34), kind=kOutput, calls=%fused_computation.7 | convolution fusion | flops 230029824 | bytes 9063936 | tf_op jit(solution)/shard_map/ltv,lpv->ltp/dot_general | solution.py:47
  73.5 1.7 %fusion.3 = f32[12,128]{1,0:T(8,128)S(1)} fusion(f32[12,128,1152]{2,1,0:T(8,128)S(1)} %get-tuple-element.20, f32[12,128]{1,0:T(8,128)S(1)} %get-tuple-element.19, pred[12,1152]{1,0:T(8,128)(4,1)S(1)} %bitcast.40), kind=kLoop, calls=%fused_computation.11 | loop fusion | flops 5306880 | bytes 7104000 | tf_op jit(solution)/shard_map/reduce_sum | solution.py:54
  75.2 2.0 %fusion.17 = bf16[12,128,64]{1,2,0:T(8,128)(2,1)S(1)} fusion(bf16[12,1152,64]{2,1,0:T(8,128)(2,1)S(1)} %bitcast.36, f32[12,128,1152]{2,1,0:T(8,128)S(1)} %get-tuple-element.20, f32[12,128]{1,0:T(8,128)S(1)} %get-tuple-element.19, pred[12,1152]{1,0:T(8,128)(4,1)S(1)} %bitcast.41, f32[12,128]{1,0:T(8,128)S(1)} %fusion.3), kind=kOutput, calls=%fused_computation.22 | convolution fusion | flops 231997440 | bytes 9070080 | tf_op jit(solution)/shard_map/uct,uth->uch/dot_general | solution.py:56
  77.2 0.1 stack.15
  77.3 0.1 stack.18
  77.4 0.1 stack.17
  77.5 0.1 stack.16
  77.6 11.6 %all_to_all.19 = bf16[4,384,64]{1,2,0:T(8,128)(2,1)S(1)} all-to-all(bf16[4,384,64]{1,2,0:T(8,128)(2,1)S(1)} %pad_maximum_fusion.2), channel_id=1, replica_groups=mesh['space'=8,'mp'=4] {'mp'}, dimensions={0} | all-to-all | bytes 393216 | tf_op jit(solution)/shard_map/all_to_all | solution.py:100
  89.2 0.0 copy-done
  89.2 1.3 %convolution_convert_fusion = bf16[384,1024]{1,0:T(8,128)(2,1)} fusion(bf16[384,256]{0,1:T(8,128)(2,1)S(1)} %bitcast.38, bf16[256,1024]{1,0:T(8,128)(2,1)S(1)} %copy-done), kind=kOutput, calls=%fused_computation.20 | convolution fusion | flops 201719808 | bytes 1507328 | tf_op jit(solution)/shard_map/dot_general | solution.py:102
  (21 shorter events, 0.4 us)
Async XLA Ops:
  0.0 89.2 %copy-start = (bf16[256,1024]{1,0:T(8,128)(2,1)S(1)}, bf16[256,1024]{1,0:T(8,128)(2,1)}, u32[]{:S(2)}) copy-start(bf16[256,1024]{1,0:T(8,128)(2,1)} %param.10) | copy-start | bytes 1572868
  0.0 5.8 %copy-start.1 = (s32[1536]{0:T(1024)S(1)}, s32[1536]{0:T(1024)}, u32[]{:S(2)}) copy-start(s32[1536]{0:T(1024)} %param.12) | copy-start | bytes 18436
  5.8 16.9 %copy-start.4 = (bf16[1024,1,192]{0,2,1:T(8,128)(2,1)S(1)}, bf16[1024,1,192]{0,2,1:T(8,128)(2,1)}, u32[]{:S(2)}) copy-start(bf16[1024,1,192]{0,2,1:T(8,128)(2,1)} %param.9) | copy-start | bytes 1179652
  5.8 16.9 %copy-start.5 = (f32[1024]{0:T(1024)S(1)}, f32[1024]{0:T(1024)}, u32[]{:S(2)}) copy-start(f32[1024]{0:T(1024)} %param.8) | copy-start | bytes 12292
  14.9 17.5 %all-to-all-start = ((s32[8,1,192]{2,1,0:T(1,128)}), s32[8,1,192]{2,1,0:T(1,128)S(1)}, u32[]{:S(2)}, u32[]{:S(2)}) async-start(s32[8,1,192]{2,1,0:T(1,128)} %all_to_all.12), calls=%async_computation | async-start | bytes 16384 | tf_op jit(solution)/shard_map/all_to_all | solution.py:76
  27.1 9.6 %copy-start.3 = (s32[12,9]{1,0:T(8,128)S(1)}, s32[12,9]{1,0:T(8,128)}, u32[]{:S(2)}) copy-start(s32[12,9]{1,0:T(8,128)} %param.13) | copy-start | bytes 1300
  32.4 16.8 %all-to-all-start.1 = ((bf16[8,192,192]{2,1,0:T(8,128)(2,1)}), bf16[8,192,192]{2,1,0:T(8,128)(2,1)S(1)}, u32[]{:S(2)}, u32[]{:S(2)}) async-start(bf16[8,192,192]{2,1,0:T(8,128)(2,1)} %bitcast.2), calls=%async_computation.1 | async-start | bytes 1572864 | tf_op jit(solution)/shard_map/all_to_all | solution.py:75
  56.5 11.2 %copy-start.2 = (bf16[1536,192]{1,0:T(8,128)(2,1)}, bf16[1536,192]{1,0:T(8,128)(2,1)S(1)}, u32[]{:S(2)}) copy-start(bf16[1536,192]{1,0:T(8,128)(2,1)S(1)} %scatter_custom_fusion) | copy-start | bytes 1769476
  56.7 8.1 %collective-permute-start = (bf16[768,128]{1,0:T(8,128)(2,1)S(1)}, bf16[768,128]{1,0:T(8,128)(2,1)S(1)}, u32[]{:S(2)}, u32[]{:S(2)}) collective-permute-start(bf16[768,128]{1,0:T(8,128)(2,1)S(1)} %get-tuple-element.13), channel_id=1, source_target_pairs={{0,4},{4,8},{8,12},{12,16},{16,20},{20,24},{24,28},{28,0},{1,5},{5... | collective-permute-start | bytes 589832 | tf_op jit(solution)/shard_map/ppermute | solution.py:17
  56.8 8.1 %collective-permute-start.1 = (bf16[768,128]{1,0:T(8,128)(2,1)S(1)}, bf16[768,128]{1,0:T(8,128)(2,1)S(1)}, u32[]{:S(2)}, u32[]{:S(2)}) collective-permute-start(bf16[768,128]{1,0:T(8,128)(2,1)S(1)} %get-tuple-element.14), channel_id=1, source_target_pairs={{4,0},{8,4},{12,8},{16,12},{20,16},{24,20},{28,24},{0,28},{5,1},{9... | collective-permute-start | bytes 589832 | tf_op jit(solution)/shard_map/ppermute | solution.py:18
  67.7 4.5 %slice-start = ((bf16[1536,192]{1,0:T(8,128)(2,1)}), bf16[1536,64]{1,0:T(8,128)(2,1)S(1)}, s32[]{:S(2)}) async-start(bf16[1536,192]{1,0:T(8,128)(2,1)} %copy-done.2), calls=%async_computation.3 | async-start | bytes 786432 | tf_op jit(solution)/shard_map/slice | solution.py:82
